TPU v7x, 32 devices: a whole 2x2x4 slice. The times are simulated.
32 devices in a mesh: group: 2 (over y), frame: 8 (over z, x), row: 2 (over core).
Axes of the slice: x: 2, y: 2, z: 4, core: 2. Of those that a mesh axis runs over, the one named last changes fastest.
Arguments:
- latents: bfloat16 [16, 8, 32, 1120], P(('group', 'frame'), 'row'), parts along dimension 0, may hold values from -24 to 24
- spatial_weights: bfloat16 [4, 10, 112, 112], replicated, may hold values from -0.5 to 0.5
- causal_weights: bfloat16 [4, 10, 112, 112], replicated, may hold values from -0.5 to 0.5
Outputs:
- updated_latents: bfloat16 [16, 8, 32, 1120], P(('group', 'frame'), None, None, 'row'), parts along dimension 0
There are 2 independent parts, one for each index of `group`. A program takes and returns all parts, laid end to end along the dimension named above; an argument that names none is the same for every part. Nothing has to cross between parts.
All inputs are finite; a program needn't handle non-finite values.
Results may differ from a plain program's by a relative error of at most 0.0047.
The roundings to bfloat16 on the way count: a program that leaves them out, or rounds other values in their place, can miss the bound.
Values may be sent and summed in bfloat16 or wider, within the bound.
No kernel may reach another device: no remote copies, remote signals or barrier semaphores. Data moves between devices by JAX's collectives and lax.ppermute only.
A program may use at most 64 MiB of HBM per device.

v0:
```python
import jax
import jax.numpy as jnp
from jax import lax
from jax.sharding import PartitionSpec as P


def prefix(x, axis, join, neutral):
    place = lax.axis_index(axis)
    gathered = lax.all_gather(x.astype(jnp.bfloat16), axis)
    state = jnp.zeros_like(x) + jnp.asarray(neutral, x.dtype)

    def one(turn, state):
        return join(state, lax.dynamic_index_in_dim(gathered, turn, 0, False).astype(x.dtype))

    return lax.fori_loop(0, place, one, state)


def normalize(frame_block):
    feat_width = frame_block.shape[-1]
    flat_rows = frame_block.reshape(-1, feat_width).astype(jnp.float32)
    normed = flat_rows * lax.rsqrt(jnp.mean(flat_rows * flat_rows, axis=-1, keepdims=True) + 1e-06)
    return normed.astype(jnp.bfloat16).reshape(frame_block.shape)


def project(normed, weights):
    head_count = weights.shape[1]
    head_size = weights.shape[2]
    normed = normed.reshape(-1, head_count, head_size)
    mapped = jnp.einsum("thd,khde->kthe", normed, weights, preferred_element_type=jnp.float32)
    queries = jax.nn.relu(mapped[0]).astype(jnp.bfloat16)
    key_rows = jax.nn.relu(mapped[1]).astype(jnp.bfloat16)
    value_rows = mapped[2].astype(jnp.bfloat16)
    gating = jax.nn.sigmoid(mapped[3])
    return (queries, key_rows, value_rows, gating)


def local_state(key_rows, value_rows):
    return jnp.einsum("thd,the->hde", key_rows, value_rows, preferred_element_type=jnp.float32)


def attend(queries, state):
    return jnp.einsum(
        "thd,hde->the", queries.astype(jnp.float32), state, precision=lax.Precision.HIGHEST
    )


def finish(frame_block, gating, attended):
    inv_rms = lax.rsqrt(jnp.mean(attended * attended, axis=-1, keepdims=True) + 1e-05)
    branch = (gating * attended * inv_rms).reshape(frame_block.shape)
    return (frame_block.astype(jnp.float32) + branch).astype(jnp.bfloat16)


def add_states(earlier, later):
    return earlier + later


def body(latents, spatial_weights, causal_weights):
    queries, key_rows, value_rows, gating = project(normalize(latents), spatial_weights)
    frame_state = lax.psum(local_state(key_rows, value_rows), "row")
    mixed_video = finish(latents, gating, attend(queries, frame_state))
    normed_c = normalize(mixed_video)
    mixed_heads, normed_heads = (
        lax.all_to_all(mixed_video, "row", split_axis=3, concat_axis=1, tiled=True),
        lax.all_to_all(normed_c, "row", split_axis=3, concat_axis=1, tiled=True),
    )
    head_part = causal_weights.shape[1] // lax.axis_size("row")
    head_start = lax.axis_index("row") * head_part
    local_weights = lax.dynamic_slice_in_dim(causal_weights, head_start, head_part, 1)
    queries, key_rows, value_rows, gating = project(normed_heads, local_weights)
    own_state = local_state(key_rows, value_rows)
    flat_state = own_state.reshape(-1, 128)
    earlier_flat = prefix(flat_state, "frame", add_states, jnp.zeros_like(flat_state))
    earlier = earlier_flat.reshape(own_state.shape)
    attended = attend(queries, earlier + own_state)
    return finish(mixed_heads, gating, attended)


def solution(mesh):
    in_specs = (P(("group", "frame"), "row", None, None), P(), P())
    out_specs = P(("group", "frame"), None, None, "row")
    return jax.shard_map(body, mesh=mesh, in_specs=in_specs, out_specs=out_specs, check_vma=False)
```

profile of v0, /device:TPU:27, one launch (start us, length us, event | category | flops | bytes accessed | tf_op | source)
XLA Modules:
  0.0 119.3 jit_solution(12640229504760504047)
XLA Ops:
  6.5 0.0 copy-start
  6.5 0.0 all-reduce.2.cloned.1.call-start
  6.5 1.6 %reshape.152 = f32[128,10,112]{2,1,0:T(8,128)S(1)} reshape(bf16[1,4,32,1120]{3,2,1,0:T(8,128)(2,1)} %param.5) | data formatting | bytes 860160 | tf_op jit(solution)/shard_map/convert_element_type | solution.py:20
  8.2 1.1 multiply_reduce_fusion
  9.3 0.1 rsqrt.36
  9.4 0.2 fusion.20
  9.6 0.0 copy-done
  9.6 0.5 convolution_bitcast_fusion.1
  10.1 1.1 fusion.24
  11.3 0.0 all-reduce.2.cloned.1.call-update
  11.3 20.5 %all-reduce.2.cloned.1.call-done = f32[10,112,112]{2,1,0:T(8,128)} async-done(((f32[10,112,112]{2,1,0:T(8,128)}), f32[10,112,112]{2,1,0:T(8,128)}) %all-reduce.2.cloned.1.call-update) | async-done | bytes 501776 | tf_op jit(solution)/shard_map/psum | solution.py:59
  31.8 1.7 %multiply_reduce_fusion.2 = (f32[128,10]{0,1:T(8,128)S(1)}, f32[128,10,112]{0,2,1:T(8,128)S(1)}) fusion(f32[10,112,112]{2,1,0:T(8,128)} %all-reduce.2.cloned.1.call-done, f32[4,128,10,112]{1,3,0,2:T(8,128)S(1)} %convolution_bitcast_fusion.1), kind=kOutput, calls=%fused_computation.40 | convolution fusion | flops 193391360 | bytes 1367040 | tf_op jit(solution)/shard_map/thd,hde->the/dot_general | solution.py:42
  33.5 1.0 fusion.18
  34.5 1.6 %copy.24 = f32[128,10,112]{2,1,0:T(8,128)S(1)} copy(f32[128,10,112]{0,2,1:T(8,128)} %fusion.18) | data formatting | bytes 1146880 | tf_op jit(solution)/shard_map/mul | solution.py:49
  36.1 0.3 reshape.147
  36.4 0.0 copy-done.2
  36.4 0.2 fusion.1
  36.6 1.4 %copy.25 = bf16[1,4,32,1120]{2,1,0,3:T(4,128)(2,1)S(1)} copy(bf16[1,4,32,1120]{3,2,1,0:T(8,128)(2,1)S(1)} %get-tuple-element.38) | data formatting | bytes 573440 | tf_op jit(solution)/shard_map/convert_element_type | solution.py:50
  38.0 0.8 fusion.2
  38.8 2.2 %copy.28 = bf16[1,4,32,1120]{2,1,0,3:T(4,128)(2,1)S(1)} copy(bf16[1,4,32,1120]{3,2,1,0:T(8,128)(2,1)} %fusion.2) | data formatting | bytes 573440 | tf_op jit(solution)/shard_map/convert_element_type | solution.py:22
  41.0 1.8 %reshape.159 = bf16[2,2,35840]{2,1,0:T(2,128)(2,1)} reshape(bf16[1120,1,4,32]{3,2,1,0:T(4,128)(2,1)S(1)} %bitcast.72) | data formatting | bytes 573440
  42.8 5.7 %all_to_all.24 = bf16[2,2,35840]{2,1,0:T(2,128)(2,1)} all-to-all(bf16[2,2,35840]{2,1,0:T(2,128)(2,1)} %reshape.159), channel_id=1, replica_groups=mesh['group'=2,'frame'=8,'row'=2] {'row'}, dimensions={0} | all-to-all | bytes 573440 | tf_op jit(solution)/shard_map/all_to_all | solution.py:64
  48.5 1.7 %reshape.160 = bf16[1120,1,4,32]{3,2,1,0:T(4,128)(2,1)S(1)} reshape(bf16[2,2,35840]{2,1,0:T(2,128)(2,1)} %all_to_all.24) | data formatting | bytes 573440
  50.2 1.4 %copy.29 = bf16[1,4,32,2,560]{4,2,1,3,0:T(8,128)(2,1)} copy(bf16[1,4,32,2,560]{2,1,4,3,0:T(4,128)(2,1)S(1)} %bitcast.73) | data formatting | bytes 573440 | tf_op jit(solution)/shard_map/all_to_all | solution.py:64
  51.5 1.4 %reshape.148 = bf16[256,5,112]{2,1,0:T(8,128)(2,1)S(1)} reshape(bf16[1,2,4,32,560]{4,3,2,1,0:T(8,128)(2,1)} %bitcast.76) | data formatting | bytes 573440 | tf_op jit(solution)/shard_map/reshape | solution.py:28
  52.9 1.6 %convolution_bitcast_fusion = f32[4,256,5,112]{1,3,0,2:T(8,128)S(1)} fusion(bf16[256,5,112,1]{2,1,0,3:T(8,128)(2,1)S(1)} %bitcast.75, bf16[4,10,112,112]{3,2,1,0:T(8,128)(2,1)} %param.7, s32[]{:T(128)S(6)} %select_n.7), kind=kOutput, calls=%fused_computation.1 | convolution fusion | flops 128450560 | bytes 3153924 | tf_op jit(solution)/shard_map/thd,khde->kthe/dot_general | solution.py:29
  54.5 1.4 %copy-done.1 = f32[4,256,5,112]{1,3,0,2:T(8,128)} copy-done((f32[4,256,5,112]{1,3,0,2:T(8,128)}, f32[4,256,5,112]{1,3,0,2:T(8,128)S(1)}, u32[]{:S(2)}) %copy-start.1) | copy-done | bytes 2293784
  55.9 0.2 fusion.46
  56.1 0.3 convert_element_type.131
  56.4 28.5 %all_gather.4 = bf16[8,490,128]{2,1,0:T(8,128)(2,1)} all-gather(bf16[1,490,128]{2,1,0:T(8,128)(2,1)S(1)} %convert_element_type.131), channel_id=1, replica_groups=mesh['group'=2,'frame'=8,'row'=2] {'frame'}, dimensions={0}, use_global_device_ids=true | all-gather | bytes 1128960 | tf_op jit(solution)/shard_map/all_gather | solution.py:9
  84.9 6.8 %while.10 = (s32[]{:T(128)}, f32[490,128]{1,0:T(8,128)S(1)}, s32[]{:T(128)}, bf16[8,490,128]{2,1,0:T(8,128)(2,1)}, s32[]{:T(128)}, /*index=5*/s32[]{:T(128)}, s32[]{:T(128)}) while((s32[]{:T(128)}, f32[490,128]{1,0:T(8,128)S(1)}, s32[]{:T(128)}, bf16[8,490,128]{2,1,0:T(8,128)(2,1)}, s32[]{:T(128)}, /*index=5*/s32[]{:T(128)}, s32[]{:T(128)}) %tuple.22), condition=%wide.region_5.6_spmd, body=%wide.region_4.5_spmd.sunk | while | flops 125445 | bytes 627315 | solution.py:15
  85.0 0.9 convert_add_fusion.2
  85.9 0.9 convert_add_fusion.2
  86.9 0.9 convert_add_fusion.2
  87.9 0.9 convert_add_fusion.2
  88.8 0.9 convert_add_fusion.2
  89.8 0.9 convert_add_fusion.2
  90.8 0.9 convert_add_fusion.2
  91.7 0.2 reshape.149
  91.9 1.5 %multiply_reduce_fusion.1 = (f32[256,5]{0,1:T(8,128)S(1)}, f32[256,5,112]{0,2,1:T(8,128)S(1)}) fusion(f32[4,256,5,112]{1,3,0,2:T(8,128)} %copy-done.1, f32[5,112,112]{2,1,0:T(8,128)S(1)} %reshape.149, f32[5,112,112]{2,1,0:T(8,128)S(1)} %get-tuple-element.42), kind=kOutput, calls=%fused_computation.39 | convolution fusion | flops 193454080 | bytes 1367040 | tf_op jit(solution)/shard_map/thd,hde->the/dot_general | solution.py:42
  93.5 2.0 %fusion.10 = f32[256,5,112]{0,2,1:T(8,128)} fusion(f32[256,5,112]{0,2,1:T(8,128)S(1)} %get-tuple-element.44, f32[4,256,5,112]{1,3,0,2:T(8,128)} %copy-done.1, f32[256,5]{0,1:T(8,128)S(1)} %add_rsqrt_fusion), kind=kLoop, calls=%fused_computation.25 | loop fusion | flops 716800 | bytes 1725440 | tf_op jit(solution)/shard_map/mul | solution.py:49
  95.5 1.5 %copy.32 = f32[256,5,112]{2,1,0:T(8,128)S(1)} copy(f32[256,5,112]{0,2,1:T(8,128)} %fusion.10) | data formatting | bytes 1146880 | tf_op jit(solution)/shard_map/mul | solution.py:49
  97.0 1.1 reshape.150
  98.0 1.1 reshape.157
  99.2 10.2 %all_to_all.25 = bf16[2,2,35840]{2,1,0:T(2,128)(2,1)S(1)} all-to-all(bf16[2,2,35840]{2,1,0:T(2,128)(2,1)S(1)} %reshape.157), channel_id=1, replica_groups=mesh['group'=2,'frame'=8,'row'=2] {'row'}, dimensions={0} | all-to-all | bytes 573440 | tf_op jit(solution)/shard_map/all_to_all | solution.py:63
  109.3 0.6 reshape.158
  109.9 0.7 copy.26
  110.6 1.9 %add_convert_fusion = bf16[1,8,32,560]{3,2,1,0:T(8,128)(2,1)} fusion(f32[1,8,32,560]{3,2,1,0:T(8,128)S(1)} %bitcast.74, f32[1,8,32,560]{3,2,1,0:T(8,128)} %reshape.150), kind=kLoop, calls=%fused_computation.9 | loop fusion | flops 286720 | bytes 1433600 | tf_op jit(solution)/shard_map/convert_element_type | solution.py:50
  (7 shorter events, 0.0 us)
Async XLA Ops:
  6.5 3.1 %copy-start = (bf16[4,10,112,112]{3,2,1,0:T(8,128)(2,1)S(1)}, bf16[4,10,112,112]{3,2,1,0:T(8,128)(2,1)}, u32[]{:S(2)}) copy-start(bf16[4,10,112,112]{3,2,1,0:T(8,128)(2,1)} %param.6) | copy-start | bytes 3010564
  6.5 25.2 %all-reduce.2.cloned.1.call-start = ((), (), s32[]{:S(2)}) async-start(), calls=%async_computation.2 | async-start | bytes 1146880 | tf_op jit(solution)/shard_map/psum | solution.py:59
  34.5 1.9 %copy-start.2 = (bf16[1,4,32,1120]{3,2,1,0:T(8,128)(2,1)S(1)}, bf16[1,4,32,1120]{3,2,1,0:T(8,128)(2,1)}, u32[]{:S(2)}) copy-start(bf16[1,4,32,1120]{3,2,1,0:T(8,128)(2,1)} %param.5) | copy-start | bytes 860164
  54.5 1.4 %copy-start.1 = (f32[4,256,5,112]{1,3,0,2:T(8,128)}, f32[4,256,5,112]{1,3,0,2:T(8,128)S(1)}, u32[]{:S(2)}) copy-start(f32[4,256,5,112]{1,3,0,2:T(8,128)S(1)} %convolution_bitcast_fusion) | copy-start | bytes 6881284
Sparse Core Ops, SparseCore 0:
  11.4 20.3 all-reduce.1
where the time goes:
time: 120 us; the launch traced here: 119 us
  blocking collectives  44.3 us (37%)
  waiting for transfers between devices  20.5 us (17%)
  local copies, waits for them, and re-layouts  20.1 us (17%)
  other arithmetic  13.8 us (12%)
  between operations  13.6 us (11%)
  matrix products  6.67 us (6%)
    all_gather x1, blocking collectives, prefix(): gathered = lax.all_gather(x.astype(jnp.bfloat16), axis)  28.5 us
    psum x1, waiting for transfers between devices, body(): frame_state = lax.psum(local_state(key_rows, value_rows), 'row')  20.5 us
    all_to_all x1, blocking collectives, body(): lax.all_to_all(mixed_video, 'row', split_axis=3, concat_axis=1, tiled=True)  10.2 us
    add x7, other arithmetic, add_states(): return earlier + later  6.6 us
    unnamed x10, local copies, waits for them, and re-layouts  6.55 us
    all_to_all x1, blocking collectives, body(): lax.all_to_all(normed_c, 'row', split_axis=3, concat_axis=1, tiled=True)  5.67 us
    dot_general x2, matrix products, attend(): jnp.einsum('thd,hde->the', queries.astype(jnp.float32), state, precision=...  3.21 us
    mul x2, local copies, waits for them, and re-layouts, finish(): branch = (gating * attended * inv_rms).reshape(frame_block.shape)  3.07 us
  transfers between devices with their start and end apart: 1, of which 1 were waited for; matrix products, arithmetic and copies ran while one was open for 0% of the time, Pallas kernels for 0%

commit v1 on v0

--- a/solution.py
+++ b/solution.py
@@ -2,6 +2,13 @@
 import jax.numpy as jnp
 from jax import lax
 from jax.sharding import PartitionSpec as P
+
+
+def swap_blocks(x, axis, split, join):
+    size = lax.axis_size(axis)
+    pieces = jnp.stack(jnp.split(x, size, axis=split), axis=0)
+    pieces = lax.all_to_all(pieces, axis, split_axis=0, concat_axis=0)
+    return jnp.concatenate(pieces, axis=join)
 
 
 def prefix(x, axis, join, neutral):
@@ -61,7 +68,7 @@
     normed_c = normalize(mixed_video)
     mixed_heads, normed_heads = (
         lax.all_to_all(mixed_video, "row", split_axis=3, concat_axis=1, tiled=True),
-        lax.all_to_all(normed_c, "row", split_axis=3, concat_axis=1, tiled=True),
+        swap_blocks(normed_c, "row", 3, 1),
     )
     head_part = causal_weights.shape[1] // lax.axis_size("row")
     head_start = lax.axis_index("row") * head_part

time: 120 us -> 110 us (0.917)
  local copies, waits for them, and re-layouts: 20.1 us -> 12.3 us
  blocking collectives: 44.3 us -> 42.6 us
    unnamed x10 -> x8, local copies, waits for them, and re-layouts: 6.55 us -> 3.07 us
    convert_element_type x1 -> x0, local copies, waits for them, and re-layouts: 2.2 us -> none  [normalize(): return normed.astype(jnp.bfloat16).reshape(frame_block.shape)]
    all_to_all x1, blocking collectives: 5.67 us -> 3.88 us  [swap_blocks(): pieces = lax.all_to_all(pieces, axis, split_axis=0, concat_axis=0)]
    reshape x1 -> x0, local copies, waits for them, and re-layouts: 1.37 us -> none  [project(): normed = normed.reshape(-1, head_count, head_size)]
    all_to_all x1 -> x0, local copies, waits for them, and re-layouts: 1.36 us -> none  [body(): lax.all_to_all(normed_c, 'row', split_axis=3, concat_axis=1, tiled=True)]
where the time goes in v1:
time: 110 us; the launch traced here: 109 us
  blocking collectives  42.6 us (39%)
  waiting for transfers between devices  20.5 us (19%)
  between operations  13.6 us (12%)
  other arithmetic  13.2 us (12%)
  local copies, waits for them, and re-layouts  12.3 us (11%)
  matrix products  6.67 us (6%)
    all_gather x1, blocking collectives, prefix(): gathered = lax.all_gather(x.astype(jnp.bfloat16), axis)  28.5 us
    psum x1, waiting for transfers between devices, body(): frame_state = lax.psum(local_state(key_rows, value_rows), 'row')  20.5 us
    all_to_all x1, blocking collectives, body(): lax.all_to_all(mixed_video, 'row', split_axis=3, concat_axis=1, tiled=True)  10.2 us
    add x7, other arithmetic, add_states(): return earlier + later  6.6 us
    all_to_all x1, blocking collectives, swap_blocks(): pieces = lax.all_to_all(pieces, axis, split_axis=0, concat_axis=0)  3.88 us
    dot_general x2, matrix products, attend(): jnp.einsum('thd,hde->the', queries.astype(jnp.float32), state, precision=...  3.21 us
    mul x2, local copies, waits for them, and re-layouts, finish(): branch = (gating * attended * inv_rms).reshape(frame_block.shape)  3.07 us
    unnamed x8, local copies, waits for them, and re-layouts  3.07 us
  transfers between devices with their start and end apart: 1, of which 1 were waited for; matrix products, arithmetic and copies ran while one was open for 0% of the time, Pallas kernels for 0%

profile of v1, /device:TPU:27, one launch (start us, length us, event | category | flops | bytes accessed | tf_op | source)
XLA Modules:
  0.0 109.0 jit_solution(2301317136984265872)
XLA Ops:
  6.5 0.0 copy-start
  6.5 0.0 all-reduce.2.cloned.1.call-start
  6.5 1.6 %reshape.147 = f32[128,10,112]{2,1,0:T(8,128)S(1)} reshape(bf16[1,4,32,1120]{3,2,1,0:T(8,128)(2,1)} %param.5) | data formatting | bytes 860160 | tf_op jit(solution)/shard_map/convert_element_type | solution.py:27
  8.2 1.1 %multiply_reduce_fusion = f32[4,32]{1,0:T(4,128)S(1)} fusion(bf16[1,4,32,1120]{3,2,1,0:T(8,128)(2,1)} %param.5), kind=kLoop, calls=%fused_computation.13 | loop fusion | flops 429952 | bytes 287232 | tf_op jit(solution)/shard_map/reduce_sum | solution.py:28
  9.3 0.1 rsqrt.36
  9.4 0.2 fusion.20
  9.6 0.0 copy-done
  9.6 0.5 convolution_bitcast_fusion.1
  10.1 1.1 %fusion.24 = f32[10,112,112]{2,1,0:T(8,128)} fusion(f32[4,128,10,112]{1,3,0,2:T(8,128)S(1)} %convolution_bitcast_fusion.1), kind=kOutput, calls=%fused_computation.46 | convolution fusion | flops 32542720 | bytes 1075200 | tf_op jit(solution)/shard_map/thd,the->hde/dot_general | solution.py:45
  11.3 0.0 all-reduce.2.cloned.1.call-update
  11.3 20.5 %all-reduce.2.cloned.1.call-done = f32[10,112,112]{2,1,0:T(8,128)} async-done(((f32[10,112,112]{2,1,0:T(8,128)}), f32[10,112,112]{2,1,0:T(8,128)}) %all-reduce.2.cloned.1.call-update) | async-done | bytes 501776 | tf_op jit(solution)/shard_map/psum | solution.py:66
  31.8 1.7 %multiply_reduce_fusion.2 = (f32[128,10]{0,1:T(8,128)S(1)}, f32[128,10,112]{0,2,1:T(8,128)S(1)}) fusion(f32[10,112,112]{2,1,0:T(8,128)} %all-reduce.2.cloned.1.call-done, f32[4,128,10,112]{1,3,0,2:T(8,128)S(1)} %convolution_bitcast_fusion.1), kind=kOutput, calls=%fused_computation.40 | convolution fusion | flops 193391360 | bytes 1367040 | tf_op jit(solution)/shard_map/thd,hde->the/dot_general | solution.py:49
  33.5 1.0 fusion.18
  34.5 0.0 copy-start.2
  34.5 1.6 %copy.23 = f32[128,10,112]{2,1,0:T(8,128)S(1)} copy(f32[128,10,112]{0,2,1:T(8,128)} %fusion.18) | data formatting | bytes 1146880 | tf_op jit(solution)/shard_map/mul | solution.py:56
  36.1 0.3 reshape.143
  36.4 0.0 copy-done.2
  36.4 0.2 fusion.1
  36.6 1.4 %copy.24 = bf16[1,4,32,1120]{2,1,0,3:T(4,128)(2,1)S(1)} copy(bf16[1,4,32,1120]{3,2,1,0:T(8,128)(2,1)S(1)} %get-tuple-element.38) | data formatting | bytes 573440 | tf_op jit(solution)/shard_map/convert_element_type | solution.py:57
  38.0 0.1 fusion.2
  38.1 0.1 slice_bitcast_fusion.1
  38.2 0.1 pad_maximum_fusion
  38.3 3.9 %all_to_all.14 = bf16[2,1,4,32,560]{4,3,2,1,0:T(8,128)(2,1)S(1)} all-to-all(bf16[2,1,4,32,560]{4,3,2,1,0:T(8,128)(2,1)S(1)} %pad_maximum_fusion), channel_id=1, replica_groups=mesh['group'=2,'frame'=8,'row'=2] {'row'}, dimensions={0} | all-to-all | bytes 573440 | tf_op jit(solution)/shard_map/all_to_all | solution.py:10
  42.2 0.4 reshape_reshape.4
  42.6 1.6 %convolution_bitcast_fusion = f32[4,256,5,112]{1,3,0,2:T(8,128)S(1)} fusion(bf16[256,5,112,1]{2,1,0,3:T(8,128)(2,1)S(1)} %bitcast.73, bf16[4,10,112,112]{3,2,1,0:T(8,128)(2,1)} %param.7, s32[]{:T(128)S(6)} %select_n.7), kind=kOutput, calls=%fused_computation.1 | convolution fusion | flops 128450560 | bytes 3153924 | tf_op jit(solution)/shard_map/thd,khde->kthe/dot_general | solution.py:36
  44.1 0.0 copy-start.1
  44.2 1.4 %copy-done.1 = f32[4,256,5,112]{1,3,0,2:T(8,128)} copy-done((f32[4,256,5,112]{1,3,0,2:T(8,128)}, f32[4,256,5,112]{1,3,0,2:T(8,128)S(1)}, u32[]{:S(2)}) %copy-start.1) | copy-done | bytes 2293784
  45.5 0.2 fusion.46
  45.8 0.3 convert_element_type.131
  46.0 28.5 %all_gather.4 = bf16[8,490,128]{2,1,0:T(8,128)(2,1)} all-gather(bf16[1,490,128]{2,1,0:T(8,128)(2,1)S(1)} %convert_element_type.131), channel_id=1, replica_groups=mesh['group'=2,'frame'=8,'row'=2] {'frame'}, dimensions={0}, use_global_device_ids=true | all-gather | bytes 1128960 | tf_op jit(solution)/shard_map/all_gather | solution.py:16
  74.6 6.8 %while.10 = (s32[]{:T(128)}, f32[490,128]{1,0:T(8,128)S(1)}, s32[]{:T(128)}, bf16[8,490,128]{2,1,0:T(8,128)(2,1)}, s32[]{:T(128)}, /*index=5*/s32[]{:T(128)}, s32[]{:T(128)}) while((s32[]{:T(128)}, f32[490,128]{1,0:T(8,128)S(1)}, s32[]{:T(128)}, bf16[8,490,128]{2,1,0:T(8,128)(2,1)}, s32[]{:T(128)}, /*index=5*/s32[]{:T(128)}, s32[]{:T(128)}) %tuple.23), condition=%wide.region_5.6_spmd, body=%wide.region_4.5_spmd.sunk | while | flops 125445 | bytes 627315 | solution.py:22
  74.6 0.9 convert_add_fusion.2
  75.6 0.9 convert_add_fusion.2
  76.6 0.9 convert_add_fusion.2
  77.5 0.9 convert_add_fusion.2
  78.5 0.9 convert_add_fusion.2
  79.5 0.9 convert_add_fusion.2
  80.4 0.9 convert_add_fusion.2
  81.4 0.2 reshape.144
  81.6 1.5 %multiply_reduce_fusion.1 = (f32[256,5]{0,1:T(8,128)S(1)}, f32[256,5,112]{0,2,1:T(8,128)S(1)}) fusion(f32[4,256,5,112]{1,3,0,2:T(8,128)} %copy-done.1, f32[5,112,112]{2,1,0:T(8,128)S(1)} %reshape.144, f32[5,112,112]{2,1,0:T(8,128)S(1)} %get-tuple-element.44), kind=kOutput, calls=%fused_computation.39 | convolution fusion | flops 193454080 | bytes 1367040 | tf_op jit(solution)/shard_map/thd,hde->the/dot_general | solution.py:49
  83.1 2.0 %fusion.10 = f32[256,5,112]{0,2,1:T(8,128)} fusion(f32[256,5,112]{0,2,1:T(8,128)S(1)} %get-tuple-element.46, f32[4,256,5,112]{1,3,0,2:T(8,128)} %copy-done.1, f32[256,5]{0,1:T(8,128)S(1)} %add_rsqrt_fusion), kind=kLoop, calls=%fused_computation.25 | loop fusion | flops 716800 | bytes 1725440 | tf_op jit(solution)/shard_map/mul | solution.py:56
  85.1 1.5 %copy.29 = f32[256,5,112]{2,1,0:T(8,128)S(1)} copy(f32[256,5,112]{0,2,1:T(8,128)} %fusion.10) | data formatting | bytes 1146880 | tf_op jit(solution)/shard_map/mul | solution.py:56
  86.6 1.1 reshape.145
  87.7 1.1 %reshape.152 = bf16[2,2,35840]{2,1,0:T(2,128)(2,1)S(1)} reshape(bf16[1120,1,4,32]{3,2,1,0:T(4,128)(2,1)S(1)} %bitcast.71) | data formatting | bytes 573440
  88.8 10.2 %all_to_all.15 = bf16[2,2,35840]{2,1,0:T(2,128)(2,1)S(1)} all-to-all(bf16[2,2,35840]{2,1,0:T(2,128)(2,1)S(1)} %reshape.152), channel_id=1, replica_groups=mesh['group'=2,'frame'=8,'row'=2] {'row'}, dimensions={0} | all-to-all | bytes 573440 | tf_op jit(solution)/shard_map/all_to_all | solution.py:70
  99.0 0.6 reshape.153
  99.5 0.7 copy.25
  100.2 1.9 %add_convert_fusion = bf16[1,8,32,560]{3,2,1,0:T(8,128)(2,1)} fusion(f32[1,8,32,560]{3,2,1,0:T(8,128)S(1)} %bitcast.72, f32[1,8,32,560]{3,2,1,0:T(8,128)} %reshape.145), kind=kLoop, calls=%fused_computation.9 | loop fusion | flops 286720 | bytes 1433600 | tf_op jit(solution)/shard_map/convert_element_type | solution.py:57
  (5 shorter events, 0.0 us)
Async XLA Ops:
  6.5 3.1 %copy-start = (bf16[4,10,112,112]{3,2,1,0:T(8,128)(2,1)S(1)}, bf16[4,10,112,112]{3,2,1,0:T(8,128)(2,1)}, u32[]{:S(2)}) copy-start(bf16[4,10,112,112]{3,2,1,0:T(8,128)(2,1)} %param.6) | copy-start | bytes 3010564
  6.5 25.2 %all-reduce.2.cloned.1.call-start = ((), (), s32[]{:S(2)}) async-start(), calls=%async_computation.2 | async-start | bytes 1146880 | tf_op jit(solution)/shard_map/psum | solution.py:66
  34.5 1.9 %copy-start.2 = (bf16[1,4,32,1120]{3,2,1,0:T(8,128)(2,1)S(1)}, bf16[1,4,32,1120]{3,2,1,0:T(8,128)(2,1)}, u32[]{:S(2)}) copy-start(bf16[1,4,32,1120]{3,2,1,0:T(8,128)(2,1)} %param.5) | copy-start | bytes 860164
  44.1 1.4 %copy-start.1 = (f32[4,256,5,112]{1,3,0,2:T(8,128)}, f32[4,256,5,112]{1,3,0,2:T(8,128)S(1)}, u32[]{:S(2)}) copy-start(f32[4,256,5,112]{1,3,0,2:T(8,128)S(1)} %convolution_bitcast_fusion) | copy-start | bytes 6881284
Sparse Core Ops, SparseCore 0:
  11.4 20.3 all-reduce.1
